TPU v7x, 32 devices: a whole 2x2x4 slice. The times are simulated.
32 devices in a mesh: leaf: 16 (over z, y, x), rows: 2 (over core).
Axes of the slice: x: 2, y: 2, z: 4, core: 2. Of those that a mesh axis runs over, the one named last changes fastest.
Arguments:
- diag_blocks: float32 [16384, 512], P(('leaf', 'rows')), as said below
- rhs: float32 [16384, 512], P(('leaf', 'rows')), may hold values from -9 to 9
- bases: float32 [16384, 384], P(('leaf', 'rows')), may hold values from -0.53033009 to 0.53033009
- coupling_one: float32 [4096, 128], P(('leaf', 'rows')), may hold values from -1 to 1
- coupling_two: float32 [1024, 128], P(('leaf', 'rows')), may hold values from -0.75 to 0.75
- coupling_top: float32 [256, 128], P(('leaf', 'rows')), may hold values from -1 to 1
Outputs:
- solution: float32 [16384, 512], P(('leaf', 'rows'))
Inputs may be any that keep to these rules, and one draw needn't show every extreme that they name: `diag_blocks`: every leaf block is symmetric with a diagonal larger than the sum of magnitudes of its row's other entries.
All inputs are finite; a program needn't handle non-finite values.
Results may differ from a plain program's by a relative error of at most 0.00025.
Values sent between devices are 32-bit elements; how exact they have to be, the bound alone decides.
No kernel may reach another device: no remote copies, remote signals or barrier semaphores. Data moves between devices by JAX's collectives and lax.ppermute only.
A program may use at most 64 MiB of HBM per device.

v0:
```python
import jax
import jax.numpy as jnp
from jax import lax
from jax.sharding import PartitionSpec as P

LEVELS = 3


def partner_2(block, axis, bit):
    count = lax.axis_size(axis)
    route = []
    for low in range(count):
        high = low | 1 << bit
        if high != low and high < count:
            route += [(low, high), (high, low)]
    return lax.ppermute(block, axis, route)


def lower_side(which_bit):
    return lax.axis_index(("leaf", "rows")) // 2**which_bit % 2 == 0


def node_rows_gather(current, bit_count):
    for which_bit in range(bit_count):
        partner = partner_2(current, ("leaf", "rows"), which_bit)
        current = jnp.where(
            lower_side(which_bit),
            jnp.concatenate([current, partner], 0),
            jnp.concatenate([partner, current], 0),
        )
    return current


def pair_sum(current, bit_count):
    for which_bit in range(bit_count):
        current = current + partner_2(current, ("leaf", "rows"), which_bit)
    return current


def top_butterfly(current, bit_count):
    for which_bit in range(bit_count):
        current = current + partner_2(current, ("leaf", "rows"), which_bit)
    return current


def per_device(diag_blocks, rhs, bases, coupling_one, coupling_two, coupling_top):
    highest = lax.Precision.HIGHEST
    block_count = lax.axis_size(("leaf", "rows"))
    all_bits = block_count.bit_length() - 1
    columns = jnp.concatenate([rhs, bases], 1)
    lower_leaf = jnp.linalg.cholesky(diag_blocks)
    solved = jax.scipy.linalg.cho_solve((lower_leaf, True), columns)
    rank_cols = bases.shape[1] // LEVELS
    rhs_cols = rhs.shape[1]
    solution = solved[:, :rhs_cols]
    basis_solved = [
        solved[:, rhs_cols + k * rank_cols : rhs_cols + (k + 1) * rank_cols] for k in range(LEVELS)
    ]
    couplings = (coupling_one, coupling_two, coupling_top)
    for level_index in range(LEVELS):
        at_top = level_index == LEVELS - 1
        node_coupling = node_rows_gather(couplings[level_index], 2 * level_index)
        remain = jnp.concatenate([solution] + basis_solved[level_index + 1 :], 1)
        basis_rows = bases[:, level_index * rank_cols : (level_index + 1) * rank_cols]
        basis_solve = basis_solved[level_index]
        weight = jnp.dot(basis_rows.T, basis_solve, precision=highest)
        projected = jnp.dot(basis_rows.T, remain, precision=highest)
        system_term = jnp.dot(
            node_coupling.T, jnp.dot(weight, node_coupling, precision=highest), precision=highest
        )
        right_term = jnp.dot(node_coupling.T, projected, precision=highest)
        term = jnp.concatenate([system_term, right_term], 1)
        if at_top:
            summed = top_butterfly(term, all_bits)
        else:
            summed = pair_sum(term, 2 * (level_index + 1))
        system = jnp.eye(rank_cols, dtype=jnp.float32) + summed[:, :rank_cols]
        lower_factor = jnp.linalg.cholesky(system)
        coeffs = jax.scipy.linalg.cho_solve((lower_factor, True), summed[:, rank_cols:])
        remain = remain - jnp.dot(
            basis_solve, jnp.dot(node_coupling, coeffs, precision=highest), precision=highest
        )
        solution = remain[:, :rhs_cols]
        for later in range(level_index + 1, LEVELS):
            start = rhs_cols + (later - level_index - 1) * rank_cols
            basis_solved[later] = remain[:, start : start + rank_cols]
    return solution


def solution(mesh):
    placed = (
        P(("leaf", "rows"), None),
        P(("leaf", "rows"), None),
        P(("leaf", "rows"), None),
        P(("leaf", "rows"), None),
        P(("leaf", "rows"), None),
        P(("leaf", "rows"), None),
    )
    return jax.shard_map(
        per_device, mesh=mesh, in_specs=placed, out_specs=P(("leaf", "rows"), None), check_vma=False
    )
```

profile of v0, /device:TPU:0, one launch (start us, length us, event | category | flops | bytes accessed | tf_op | source)
XLA Modules:
  0.0 353.7 jit_solution(14262337511811247659)
XLA Ops:
  1.9 11.7 %cholesky.138 = f32[128,128]{1,0:T(8,128)S(1)} custom-call(f32[128,128]{1,0:T(8,128)S(1)} %cholesky.392), custom_call_target="Cholesky" | custom-call | tf_op jit(solution)/shard_map/jit(cholesky)/cholesky | solution.py:51
  13.7 9.8 %custom-call.57 = f32[1,128,128]{1,2,0:T(8,128)S(1)} custom-call(f32[1,128,128]{2,1,0:T(8,128)S(1)} %get-tuple-element.33), custom_call_target="InvertDiagBlocksLowerTriangular" | custom-call | tf_op jit(solution)/shard_map/jit(cholesky)/cholesky | solution.py:51
  24.3 11.7 %cholesky.280 = f32[128,128]{1,0:T(8,128)S(1)} custom-call(f32[128,128]{1,0:T(8,128)S(1)} %cholesky.396), custom_call_target="Cholesky" | custom-call | tf_op jit(solution)/shard_map/jit(cholesky)/cholesky | solution.py:51
  36.0 10.0 %custom-call.58 = f32[1,128,128]{1,2,0:T(8,128)S(1)} custom-call(f32[1,128,128]{2,1,0:T(8,128)S(1)} %get-tuple-element.30), custom_call_target="InvertDiagBlocksLowerTriangular" | custom-call | tf_op jit(solution)/shard_map/jit(cholesky)/cholesky | solution.py:51
  46.7 11.7 %cholesky.301 = f32[128,128]{1,0:T(8,128)S(1)} custom-call(f32[128,128]{1,0:T(8,128)S(1)} %cholesky.401), custom_call_target="Cholesky" | custom-call | tf_op jit(solution)/shard_map/jit(cholesky)/cholesky | solution.py:51
  59.2 9.8 %custom-call.59 = f32[1,128,128]{1,2,0:T(8,128)S(1)} custom-call(f32[1,128,128]{2,1,0:T(8,128)S(1)} %get-tuple-element.27), custom_call_target="InvertDiagBlocksLowerTriangular" | custom-call | tf_op jit(solution)/shard_map/jit(cholesky)/cholesky | solution.py:51
  69.6 11.7 %cholesky.318 = f32[128,128]{1,0:T(8,128)S(1)} custom-call(f32[128,128]{1,0:T(8,128)S(1)} %convolution_subtract_fusion.9), custom_call_target="Cholesky" | custom-call | tf_op jit(solution)/shard_map/jit(cholesky)/cholesky | solution.py:51
  85.4 10.2 %triangular_solve.165 = s32[4,2]{0,1:T(2,128)S(1)} broadcast(s32[4]{0:T(128)S(1)} %iota_multiply_fusion), dimensions={0} | broadcast | bytes 48 | tf_op jit(solution)/shard_map/jit(_cho_solve)/triangular_solve | solution.py:52
  95.6 10.5 %while.1 = (s32[]{:T(128)}, f32[512,512]{1,0:T(8,128)S(1)}, s32[4,2]{0,1:T(2,128)S(1)}, f32[4,128,128]{2,1,0:T(8,128)}, s32[]{:T(128)}) while((s32[]{:T(128)}, f32[512,512]{1,0:T(8,128)S(1)}, s32[4,2]{0,1:T(2,128)S(1)}, f32[4,128,128]{2,1,0:T(8,128)}, s32[]{:T(128)}) %tuple.28), condition=%wide.while_cond, body=%wide.while_body.sunk | while | flops 2 | bytes 132705 | solution.py:52
  96.3 2.0 bitcast_dynamic-update-slice_fusion.2
  107.1 40.1 %custom-call.60 = f32[4,128,128]{1,2,0:T(8,128)S(1)} custom-call(f32[4,128,128]{2,1,0:T(8,128)} %get-tuple-element.13), custom_call_target="InvertDiagBlocksLowerTriangular" | custom-call | tf_op jit(solution)/shard_map/jit(_cho_solve)/triangular_solve | solution.py:52
  158.5 2.6 fusion.48
  166.2 2.9 collective-permute-start.1
  170.2 10.3 %collective-permute-done.1 = f32[128,896]{1,0:T(8,128)} collective-permute-done((f32[128,896]{1,0:T(8,128)}, f32[128,896]{1,0:T(8,128)}, u32[]{:S(2)}, u32[]{:S(2)}) %collective-permute-start.1) | collective-permute-done | bytes 458784 | tf_op jit(solution)/shard_map/ppermute | solution.py:16
  185.5 12.5 %cholesky.361 = f32[128,128]{1,0:T(8,128)S(1)} custom-call(f32[128,128]{1,0:T(8,128)} %copy.11), custom_call_target="Cholesky" | custom-call | tf_op jit(solution)/shard_map/jit(cholesky)/cholesky | solution.py:78
  200.0 10.6 %custom-call.61 = f32[1,128,128]{1,2,0:T(8,128)S(1)} custom-call(f32[1,128,128]{2,1,0:T(8,128)} %fusion.61), custom_call_target="InvertDiagBlocksLowerTriangular" | custom-call | tf_op jit(solution)/shard_map/jit(_cho_solve)/triangular_solve | solution.py:79
  215.1 2.4 fusion.19
  222.2 9.4 %collective-permute-done.5 = f32[128,768]{1,0:T(8,128)S(1)} collective-permute-done((f32[128,768]{1,0:T(8,128)S(1)}, f32[128,768]{1,0:T(8,128)S(1)}, u32[]{:S(2)}, u32[]{:S(2)}) %collective-permute-start.5) | collective-permute-done | bytes 393248 | tf_op jit(solution)/shard_map/ppermute | solution.py:16
  233.5 8.6 %collective-permute-done.6 = f32[128,768]{1,0:T(8,128)S(1)} collective-permute-done((f32[128,768]{1,0:T(8,128)S(1)}, f32[128,768]{1,0:T(8,128)S(1)}, u32[]{:S(2)}, u32[]{:S(2)}) %collective-permute-start.6) | collective-permute-done | bytes 393248 | tf_op jit(solution)/shard_map/ppermute | solution.py:16
  246.7 2.2 collective-permute-done.9
  250.3 2.2 collective-permute-done.10
  253.1 11.7 %cholesky.372 = f32[128,128]{1,0:T(8,128)S(1)} custom-call(f32[128,128]{1,0:T(8,128)S(1)} %copy.14), custom_call_target="Cholesky" | custom-call | tf_op jit(solution)/shard_map/jit(cholesky)/cholesky | solution.py:78
  266.2 9.8 %custom-call.62 = f32[1,128,128]{1,2,0:T(8,128)S(1)} custom-call(f32[1,128,128]{2,1,0:T(8,128)S(1)} %fusion.62), custom_call_target="InvertDiagBlocksLowerTriangular" | custom-call | tf_op jit(solution)/shard_map/jit(_cho_solve)/triangular_solve | solution.py:79
  277.3 2.1 convolution_subtract_fusion.1
  279.4 2.0 fusion.21
  286.6 8.0 %collective-permute-done.13 = f32[128,640]{1,0:T(8,128)S(1)} collective-permute-done((f32[128,640]{1,0:T(8,128)S(1)}, f32[128,640]{1,0:T(8,128)S(1)}, u32[]{:S(2)}, u32[]{:S(2)}) %collective-permute-start.13) | collective-permute-done | bytes 327712 | tf_op jit(solution)/shard_map/ppermute | solution.py:16
  296.5 7.2 %collective-permute-done.14 = f32[128,640]{1,0:T(8,128)S(1)} collective-permute-done((f32[128,640]{1,0:T(8,128)S(1)}, f32[128,640]{1,0:T(8,128)S(1)}, u32[]{:S(2)}, u32[]{:S(2)}) %collective-permute-start.14) | collective-permute-done | bytes 327712 | tf_op jit(solution)/shard_map/ppermute | solution.py:16
  305.6 6.3 %collective-permute-done.15 = f32[128,640]{1,0:T(8,128)S(1)} collective-permute-done((f32[128,640]{1,0:T(8,128)S(1)}, f32[128,640]{1,0:T(8,128)S(1)}, u32[]{:S(2)}, u32[]{:S(2)}) %collective-permute-start.15) | collective-permute-done | bytes 327712 | tf_op jit(solution)/shard_map/ppermute | solution.py:16
  311.9 2.8 collective-permute-start.16
  314.7 12.5 %collective-permute-done.16 = f32[128,640]{1,0:T(8,128)S(1)} collective-permute-done((f32[128,640]{1,0:T(8,128)S(1)}, f32[128,640]{1,0:T(8,128)S(1)}, u32[]{:S(2)}, u32[]{:S(2)}) %collective-permute-start.16) | collective-permute-done | bytes 327712 | tf_op jit(solution)/shard_map/ppermute | solution.py:16
  327.5 11.7 %cholesky.383 = f32[128,128]{1,0:T(8,128)S(1)} custom-call(f32[128,128]{1,0:T(8,128)S(1)} %copy.17), custom_call_target="Cholesky" | custom-call | tf_op jit(solution)/shard_map/jit(cholesky)/cholesky | solution.py:78
  340.5 9.8 %custom-call.63 = f32[1,128,128]{1,2,0:T(8,128)S(1)} custom-call(f32[1,128,128]{2,1,0:T(8,128)S(1)} %fusion.63), custom_call_target="InvertDiagBlocksLowerTriangular" | custom-call | tf_op jit(solution)/shard_map/jit(_cho_solve)/triangular_solve | solution.py:79
  (159 shorter events, 73.7 us)
Async XLA Ops:
  0.0 162.1 %copy-start = (f32[128,128]{1,0:T(8,128)S(1)}, f32[128,128]{1,0:T(8,128)}, u32[]{:S(2)}) copy-start(f32[128,128]{1,0:T(8,128)} %param.10) | copy-start | bytes 196612
  0.0 1.7 copy-start.4
  85.4 63.1 %copy-start.1 = (f32[512,384]{1,0:T(8,128)S(1)}, f32[512,384]{1,0:T(8,128)}, u32[]{:S(2)}) copy-start(f32[512,384]{1,0:T(8,128)} %param.9) | copy-start | bytes 2359300
  106.1 1.0 copy-start.2
  148.5 1.2 copy-start.3
  158.5 2.7 copy-start.6
  162.1 6.9 %copy-start.8 = (f32[32,128]{1,0:T(8,128)S(1)}, f32[32,128]{1,0:T(8,128)}, u32[]{:S(2)}) copy-start(f32[32,128]{1,0:T(8,128)} %param.11) | copy-start | bytes 49156
  163.3 2.0 collective-permute-start
  166.2 14.3 %collective-permute-start.1 = (f32[128,896]{1,0:T(8,128)}, f32[128,896]{1,0:T(8,128)}, u32[]{:S(2)}, u32[]{:S(2)}) collective-permute-start(f32[128,896]{1,0:T(8,128)} %fusion.105), channel_id=1, source_target_pairs={{0,2},{2,0},{1,3},{3,1},{4,6},{6,4},{5,7},{7,5},{8,10},{10,8},{9,1... | collective-permute-start | bytes 1376264 | tf_op jit(solution)/shard_map/ppermute | solution.py:16
  169.0 1.2 collective-permute-start.2
  170.2 47.2 %collective-permute-start.3 = (f32[64,128]{1,0:T(8,128)S(1)}, f32[64,128]{1,0:T(8,128)S(1)}, u32[]{:S(2)}, u32[]{:S(2)}) collective-permute-start(f32[64,128]{1,0:T(8,128)S(1)} %maximum_select_fusion.2), channel_id=1, source_target_pairs={{0,2},{2,0},{1,3},{3,1},{4,6},{6,4},{5,7},{7,5},{8,10},{10,8},{9,1... | collective-permute-start | bytes 98312 | tf_op jit(solution)/shard_map/ppermute | solution.py:16
  210.6 1.8 copy-start.7
  213.9 1.2 copy-start.5
  218.6 25.4 %copy-start.9 = (f32[8,128]{1,0:T(8,128)S(1)}, f32[8,128]{1,0:T(8,128)}, u32[]{:S(2)}) copy-start(f32[8,128]{1,0:T(8,128)} %param.12) | copy-start | bytes 12292
  218.6 1.8 collective-permute-start.4
  220.4 11.2 %collective-permute-start.5 = (f32[128,768]{1,0:T(8,128)S(1)}, f32[128,768]{1,0:T(8,128)S(1)}, u32[]{:S(2)}, u32[]{:S(2)}) collective-permute-start(f32[128,768]{1,0:T(8,128)S(1)} %fusion.104), channel_id=1, source_target_pairs={{0,2},{2,0},{1,3},{3,1},{4,6},{6,4},{5,7},{7,5},{8,10},{10,8},{9,1... | collective-permute-start | bytes 1179656 | tf_op jit(solution)/shard_map/ppermute | solution.py:16
  231.7 10.4 %collective-permute-start.6 = (f32[128,768]{1,0:T(8,128)S(1)}, f32[128,768]{1,0:T(8,128)S(1)}, u32[]{:S(2)}, u32[]{:S(2)}) collective-permute-start(f32[128,768]{1,0:T(8,128)S(1)} %add.146), channel_id=1, source_target_pairs={{0,4},{4,0},{1,5},{5,1},{2,6},{6,2},{3,7},{7,3},{8,12},{12,8},{9,1... | collective-permute-start | bytes 1179656 | tf_op jit(solution)/shard_map/ppermute | solution.py:16
  242.1 10.7 %collective-permute-start.7 = (f32[128,768]{1,0:T(8,128)S(1)}, f32[128,768]{1,0:T(8,128)S(1)}, u32[]{:S(2)}, u32[]{:S(2)}) collective-permute-start(f32[128,768]{1,0:T(8,128)S(1)} %add.147), channel_id=1, source_target_pairs={{0,8},{8,0},{1,9},{9,1},{2,10},{10,2},{3,11},{11,3},{4,12},{12,4},... | collective-permute-start | bytes 1179656 | tf_op jit(solution)/shard_map/ppermute | solution.py:16
  244.0 1.2 collective-permute-start.8
  245.2 3.7 %collective-permute-start.9 = (f32[16,128]{1,0:T(8,128)S(1)}, f32[16,128]{1,0:T(8,128)S(1)}, u32[]{:S(2)}, u32[]{:S(2)}) collective-permute-start(f32[16,128]{1,0:T(8,128)S(1)} %maximum_select_fusion.5), channel_id=1, source_target_pairs={{0,2},{2,0},{1,3},{3,1},{4,6},{6,4},{5,7},{7,5},{8,10},{10,8},{9,1... | collective-permute-start | bytes 24584 | tf_op jit(solution)/shard_map/ppermute | solution.py:16
  248.8 3.7 %collective-permute-start.10 = (f32[32,128]{1,0:T(8,128)S(1)}, f32[32,128]{1,0:T(8,128)S(1)}, u32[]{:S(2)}, u32[]{:S(2)}) collective-permute-start(f32[32,128]{1,0:T(8,128)S(1)} %maximum_select_fusion.4), channel_id=1, source_target_pairs={{0,4},{4,0},{1,5},{5,1},{2,6},{6,2},{3,7},{7,3},{8,12},{12,8},{9,1... | collective-permute-start | bytes 49160 | tf_op jit(solution)/shard_map/ppermute | solution.py:16
  252.6 29.5 %collective-permute-start.11 = (f32[64,128]{1,0:T(8,128)S(1)}, f32[64,128]{1,0:T(8,128)S(1)}, u32[]{:S(2)}, u32[]{:S(2)}) collective-permute-start(f32[64,128]{1,0:T(8,128)S(1)} %maximum_select_fusion.3), channel_id=1, source_target_pairs={{0,8},{8,0},{1,9},{9,1},{2,10},{10,2},{3,11},{11,3},{4,12},{12,4},... | collective-permute-start | bytes 98312 | tf_op jit(solution)/shard_map/ppermute | solution.py:16
  283.1 1.7 collective-permute-start.12
  284.8 9.8 %collective-permute-start.13 = (f32[128,640]{1,0:T(8,128)S(1)}, f32[128,640]{1,0:T(8,128)S(1)}, u32[]{:S(2)}, u32[]{:S(2)}) collective-permute-start(f32[128,640]{1,0:T(8,128)S(1)} %fusion.103), channel_id=1, source_target_pairs={{0,2},{2,0},{1,3},{3,1},{4,6},{6,4},{5,7},{7,5},{8,10},{10,8},{9,1... | collective-permute-start | bytes 983048 | tf_op jit(solution)/shard_map/ppermute | solution.py:16
  294.7 9.0 %collective-permute-start.14 = (f32[128,640]{1,0:T(8,128)S(1)}, f32[128,640]{1,0:T(8,128)S(1)}, u32[]{:S(2)}, u32[]{:S(2)}) collective-permute-start(f32[128,640]{1,0:T(8,128)S(1)} %add.153), channel_id=1, source_target_pairs={{0,4},{4,0},{1,5},{5,1},{2,6},{6,2},{3,7},{7,3},{8,12},{12,8},{9,1... | collective-permute-start | bytes 983048 | tf_op jit(solution)/shard_map/ppermute | solution.py:16
  303.7 8.2 %collective-permute-start.15 = (f32[128,640]{1,0:T(8,128)S(1)}, f32[128,640]{1,0:T(8,128)S(1)}, u32[]{:S(2)}, u32[]{:S(2)}) collective-permute-start(f32[128,640]{1,0:T(8,128)S(1)} %add.154), channel_id=1, source_target_pairs={{0,8},{8,0},{1,9},{9,1},{2,10},{10,2},{3,11},{11,3},{4,12},{12,4},... | collective-permute-start | bytes 983048 | tf_op jit(solution)/shard_map/ppermute | solution.py:16
  311.9 15.3 %collective-permute-start.16 = (f32[128,640]{1,0:T(8,128)S(1)}, f32[128,640]{1,0:T(8,128)S(1)}, u32[]{:S(2)}, u32[]{:S(2)}) collective-permute-start(f32[128,640]{1,0:T(8,128)S(1)} %add.155), channel_id=1, source_target_pairs={{0,16},{16,0},{1,17},{17,1},{2,18},{18,2},{3,19},{19,3},{4,20},{20... | collective-permute-start | bytes 983048 | tf_op jit(solution)/shard_map/ppermute | solution.py:16
where the time goes:
time: 358 us; the launch traced here: 354 us
  other arithmetic  194 us (54%)
  waiting for transfers between devices  73.7 us (21%)
  matrix products  32.9 us (9%)
  local copies, waits for them, and re-layouts  28.9 us (8%)
  starting transfers between devices  20.6 us (6%)
    another operation x14, other arithmetic, per_device(): lower_leaf = jnp.linalg.cholesky(diag_blocks)  78.7 us
    ppermute x17, waiting for transfers between devices, partner_2(): return lax.ppermute(block, axis, route)  73.7 us
    another operation x4, other arithmetic, per_device(): solved = jax.scipy.linalg.cho_solve((lower_leaf, True), columns)  40.4 us
    another operation x9, other arithmetic, per_device(): lower_factor = jnp.linalg.cholesky(system)  38 us
    another operation x6, other arithmetic, per_device(): jax.scipy.linalg.cho_solve((lower_factor, True), summed[:, rank_cols:])  32.8 us
    ppermute x17, starting transfers between devices, partner_2(): return lax.ppermute(block, axis, route)  20.6 us
    another operation x12, local copies, waits for them, and re-layouts  10.5 us
    another operation x1, local copies, waits for them, and re-layouts, per_device(): solved = jax.scipy.linalg.cho_solve((lower_leaf, True), columns)  10.2 us
  transfers between devices with their start and end apart: 17, of which 14 were waited for; matrix products, arithmetic and copies ran while one was open for 19% of the time, Pallas kernels for 0%

commit v1 on v0

v1 whole, which is shorter than its diff:
```python
import functools

import jax
import jax.numpy as jnp
from jax import lax
from jax.experimental import pallas as pl
from jax.experimental.pallas import tpu as pltpu
from jax.sharding import PartitionSpec as P

AXES = ("leaf", "rows")
F32 = jnp.float32
BF16 = jnp.bfloat16
VMEM = pl.BlockSpec(memory_space=pltpu.VMEM)
FALLBACK_STEPS = 32


def partner(block, flip):
    count = lax.axis_size(AXES)
    return lax.ppermute(block, AXES, [(low, low ^ flip) for low in range(count)])


def split(value):
    high = value.astype(BF16)
    return high, (value - high.astype(F32)).astype(BF16)


def dot1(left, right):
    return jnp.dot(left, right, preferred_element_type=F32)


def dot3(left, right):
    left_high, left_low = split(left)
    right_high, right_low = split(right)
    return dot1(left_high, right_high) + (dot1(left_high, right_low) + dot1(left_low, right_high))


def dot6(left, right):
    return jnp.dot(left, right, preferred_element_type=F32, precision=lax.Precision.HIGHEST)


def eye(order):
    rows = lax.broadcasted_iota(jnp.int32, (order, order), 0)
    cols = lax.broadcasted_iota(jnp.int32, (order, order), 1)
    return rows == cols


def inverse_into(out_ref, matrix, least, most, short_steps):
    order = matrix.shape[0]
    unit = jnp.where(eye(order), 1.0, 0.0).astype(F32)
    high, low = split(matrix)
    floor = least / most
    scale = 2.0 / (most + least)
    estimate = scale * (2.0 * unit - scale * matrix)
    floor = 4.0 * floor / ((1.0 + floor) * (1.0 + floor))
    for _ in range(short_steps):
        scale = 2.0 / (1.0 + floor)
        short = estimate.astype(BF16)
        rest = unit - scale * dot1(high, short)
        estimate = scale * (short.astype(F32) + dot1(short, rest.astype(BF16)))
        floor = 4.0 * floor / ((1.0 + floor) * (1.0 + floor))
    short = estimate.astype(BF16)
    rest = unit - (dot1(high, short) + dot1(low, short))
    estimate = short.astype(F32) + dot1(short, rest.astype(BF16))
    est_high, est_low = split(estimate)
    rest = unit - (dot1(high, est_high) + (dot1(high, est_low) + dot1(low, est_high)))
    out_ref[...] = estimate + dot1(est_high, rest.astype(BF16))
    size = jnp.sum(rest * rest)

    @pl.when(jnp.logical_not(size < 1e-6))
    def _():
        first = 2.0 / (most + least)
        out_ref[...] = first * (2.0 * unit - first * matrix)

        def step(_, floor):
            scale = 2.0 / (1.0 + floor)
            current = out_ref[...]
            left = unit - scale * dot6(matrix, current)
            out_ref[...] = scale * (current + dot6(current, left))
            return 4.0 * floor / ((1.0 + floor) * (1.0 + floor))

        start = least / most
        start = 4.0 * start / ((1.0 + start) * (1.0 + start))
        lax.fori_loop(0, FALLBACK_STEPS, step, start)


def leaf_kernel(rank, d_ref, u_ref, g_ref, dinv_ref, yut_ref, w_ref, inv_ref):
    order = d_ref.shape[0]
    core = lax.axis_index("rows")
    block = d_ref[...]
    diag_row = jnp.sum(jnp.where(eye(order), block, 0.0), axis=0, keepdims=True)
    diag_col = jnp.sum(jnp.where(eye(order), block, 0.0), axis=1, keepdims=True)
    row_total = jnp.sum(jnp.abs(block), axis=1, keepdims=True)
    least = jnp.min((2.0 * diag_col - row_total) / diag_col, axis=0, keepdims=True)
    least = jnp.maximum(least, 2.0**-22)
    scale_row = lax.rsqrt(diag_row)
    scale_col = lax.rsqrt(diag_col)
    inverse_into(inv_ref, block * scale_row * scale_col, least, 2.0 - least, 5)
    inverse = inv_ref[...] * scale_row * scale_col
    dinv_ref[...] = inverse
    first = dot3(u_ref[:, :rank], g_ref[...])
    basis = jnp.concatenate([first, u_ref[:, rank:]], axis=1)
    solved = dot3(basis.T, inverse)
    yut_ref[...] = solved
    weight = dot3(solved, basis)
    part = lambda i, j: weight[i * rank : (i + 1) * rank, j * rank : (j + 1) * rank]
    w_ref[core] = jnp.concatenate([part(0, 0), part(0, 1), part(0, 2)], axis=0)
    w_ref[1 - core] = jnp.concatenate([part(1, 1), part(1, 2), part(2, 2)], axis=0)


def project_kernel(yut_ref, rhs_ref, p_ref):
    spot = lax.axis_index(AXES) % 4
    width = rhs_ref.shape[1] // 4
    solved = yut_ref[...]
    for chunk in range(4):
        start = pl.multiple_of((spot ^ chunk) * width, width)
        p_ref[chunk] = dot3(solved, rhs_ref[:, pl.ds(start, width)])


def solve_kernel(dinv_ref, rhs_ref, out_ref):
    out_ref[...] = dot3(dinv_ref[...], rhs_ref[...])


def refine(matrix, inverse, right):
    found = dot3(inverse, right)
    return found + dot1(inverse.astype(BF16), (right - dot3(matrix, found)).astype(BF16))


def lift_kernel_matrix(rank, count, mine_ref, other_ref, *refs):
    pieces, (half_ref, inv_ref, mat_ref, found_ref, link_ref, next_ref) = refs[:4], refs[4:]
    core = lax.axis_index("rows")
    spot = lax.axis_index(AXES) // (4 if count == 2 else 1) % 4
    mine, other = mine_ref[...], other_ref[...]
    both = jnp.concatenate(
        [jnp.where(core == 0, mine, other), jnp.where(core == 0, other, mine)], axis=0
    )
    part = lambda k: both[k * rank : (k + 1) * rank]
    unit = jnp.where(eye(rank), 1.0, 0.0).astype(F32)
    matrix = unit + part(0)
    most = jnp.max(jnp.sum(jnp.abs(matrix), axis=1, keepdims=True), axis=0, keepdims=True)
    inverse_into(inv_ref, matrix, jnp.ones_like(most), most, 4)
    mat_ref[...] = matrix
    links = [part(k) for k in range(1, count)]
    link = jnp.concatenate(links, axis=1)
    link_ref[...] = link
    found = refine(matrix, inv_ref[...], link)
    found_ref[...] = found
    height = pieces[0].shape[0]
    for chunk in range(4):
        start = pl.multiple_of((spot ^ chunk) * height, height)
        next_ref[pl.ds(start, height), :] = pieces[chunk][...]
    below = dot3(link.T, found)
    cell = lambda i, j: below[i * rank : (i + 1) * rank, j * rank : (j + 1) * rank]
    coupling = next_ref[...]
    turned = coupling.T
    if count == 3:
        top = dot3(dot3(turned, part(3) - cell(0, 0)), coupling)
        side = dot3(turned, part(4) - cell(0, 1))
        last = part(5) - cell(1, 1)
        whole = jnp.concatenate([top, side, last], axis=0)
        size = whole.shape[0] // 2
        half_ref[...] = jnp.where(core == 0, whole[:size], whole[size:])
    else:
        half_ref[...] = dot3(dot3(turned, part(2) - cell(0, 0)), coupling)


def lift_kernel_rhs(rank, p_ref, inv_ref, mat_ref, link_ref, next_ref, found_ref, up_ref):
    right = p_ref[...]
    found = refine(mat_ref[...], inv_ref[...], right[:rank])
    found_ref[...] = found
    rest = right[rank:] - dot3(link_ref[...].T, found)
    first = dot3(next_ref[...].T, rest[:rank])
    up_ref[:rank] = first
    if rest.shape[0] > rank:
        up_ref[rank:] = rest[rank:]


def top_kernel(rank, w_ref, p_ref, g1_ref, g2_ref, f0r_ref, f0_ref, f1r_ref, f1_ref, c_ref, inv_ref):
    unit = jnp.where(eye(rank), 1.0, 0.0).astype(F32)
    matrix = unit + w_ref[...]
    most = jnp.max(jnp.sum(jnp.abs(matrix), axis=1, keepdims=True), axis=0, keepdims=True)
    inverse_into(inv_ref, matrix, jnp.ones_like(most), most, 4)
    coeff_two = dot3(g2_ref[...], refine(matrix, inv_ref[...], p_ref[...]))
    coeff_one = dot3(g1_ref[...], f1r_ref[...] - dot3(f1_ref[...], coeff_two))
    lower = jnp.concatenate([coeff_one, coeff_two], axis=0)
    c_ref[:rank] = f0r_ref[...] - dot3(f0_ref[...], lower)
    c_ref[rank:] = lower


def finish_kernel(y_ref, yut_ref, c0_ref, c2_ref, c1_ref, out_ref):
    spot = lax.axis_index(AXES) % 4
    width = c0_ref.shape[1]
    solved = yut_ref[...].T
    coeffs = (c0_ref[...], c1_ref[0], c2_ref[...], c1_ref[1])
    for chunk in range(4):
        cols = pl.ds(pl.multiple_of((spot ^ chunk) * width, width), width)
        out_ref[:, cols] = y_ref[:, cols] - dot3(solved, coeffs[chunk])


def call(kernel, outs, scratch=(), name=None):
    return lambda *args: pl.pallas_call(
        kernel,
        out_shape=outs,
        in_specs=[VMEM] * len(args),
        out_specs=jax.tree.map(lambda _: VMEM, outs),
        scratch_shapes=list(scratch),
        name=name,
    )(*args)


def shape(*sizes):
    return jax.ShapeDtypeStruct(sizes, F32)


def per_device(diag_blocks, rhs, bases, coupling_one, coupling_two, coupling_top):
    rank = coupling_one.shape[1]
    order, rhs_cols = rhs.shape
    all_cols = bases.shape[1]
    width = rhs_cols // 4
    all_bits = lax.axis_size(AXES).bit_length() - 1

    two_rows = coupling_two.shape[0]
    packed = jnp.concatenate([coupling_two, coupling_top], axis=0)
    around = [packed] + [partner(packed, k) for k in (1, 2, 3)]
    one_pieces = [piece[:two_rows] for piece in around]

    dinv, solved_t, weights = call(
        functools.partial(leaf_kernel, rank),
        (shape(order, order), shape(all_cols, order), shape(2, 3 * rank, rank)),
        [pltpu.VMEM((order, order), F32)],
        "leaf",
    )(diag_blocks, bases, coupling_one)

    mine = weights[0] + partner(weights[1], 1)
    projected = call(project_kernel, shape(4, all_cols, width), name="project")(solved_t, rhs)
    mine = mine + partner(mine, 2)
    sent = jnp.stack([projected[1], projected[3]])
    got = partner(sent, 1)
    other = partner(mine, 1)
    solution_part = call(solve_kernel, shape(order, rhs_cols), name="solve")(dinv, rhs)
    right = projected[0] + got[0] + partner(projected[2] + got[1], 2)

    top_pieces = [piece[two_rows:] for piece in around]
    spot = lax.axis_index(AXES) % 4
    stacked = jnp.stack(top_pieces)
    ordered = jnp.concatenate([stacked[spot ^ k] for k in range(4)], axis=0)
    top_around = [ordered] + [partner(ordered, k) for k in (4, 8, 12)]

    half, inv0, mat0, found0, link0, coup1 = call(
        functools.partial(lift_kernel_matrix, rank, 3),
        (shape(3 * rank // 2, rank), shape(rank, rank), shape(rank, rank), shape(rank, 2 * rank), shape(rank, 2 * rank), shape(rank, rank)),
        name="lift_zero",
    )(mine, other, *one_pieces)
    half = half + partner(half, 4)
    found0r, right = call(
        functools.partial(lift_kernel_rhs, rank),
        (shape(rank, width), shape(2 * rank, width)),
        name="lift_zero_rhs",
    )(right, inv0, mat0, link0, coup1)
    half = half + partner(half, 8)
    right = right + partner(right, 4)
    other = partner(half, 1)
    right = right + partner(right, 8)

    last, inv1, mat1, found1, link1, coup2 = call(
        functools.partial(lift_kernel_matrix, rank, 2),
        (shape(rank, rank), shape(rank, rank), shape(rank, rank), shape(rank, rank), shape(rank, rank), shape(rank, rank)),
        name="lift_one",
    )(half, other, *top_around)
    found1r, right = call(
        functools.partial(lift_kernel_rhs, rank),
        (shape(rank, width), shape(rank, width)),
        name="lift_one_rhs",
    )(right, inv1, mat1, link1, coup2)
    for bit in range(4, all_bits):
        last = last + partner(last, 1 << bit)
        right = right + partner(right, 1 << bit)
    coeffs = call(
        functools.partial(top_kernel, rank),
        shape(all_cols, width),
        [pltpu.VMEM((rank, rank), F32)],
        "top",
    )(last, right, coup1, coup2, found0r, found0, found1r, found1)
    coeffs_x = partner(coeffs, 2)
    coeffs_core = partner(jnp.stack([coeffs, coeffs_x]), 1)
    return call(finish_kernel, shape(order, rhs_cols), name="finish")(
        solution_part, solved_t, coeffs, coeffs_x, coeffs_core
    )


def solution(mesh):
    placed = (P(AXES, None),) * 6
    return jax.shard_map(
        per_device, mesh=mesh, in_specs=placed, out_specs=P(AXES, None), check_vma=False
    )
```

time: 358 us -> 235 us (0.66); the launches traced: 354 us -> 235 us
  other arithmetic: 194 us -> 4.63 us
  Pallas kernels: 0 us -> 161 us
  waiting for transfers between devices: 73.7 us -> 29.2 us
  matrix products: 32.9 us -> 0 us
  local copies, waits for them, and re-layouts: 28.9 us -> 7.29 us
  starting transfers between devices: 20.6 us -> 32.7 us
    another operation x33 -> x3, other arithmetic: 190 us -> 1.05 us  [the longest x1 1.02 us: per_device(): coeffs_core = partner(jnp.stack([coeffs, coeffs_x]), 1)]
    pallas_call x0 -> x9, Pallas kernels: none -> 161 us  [call(): pl.pallas_call(kernel, out_shape=outs, in_specs=[VMEM] * len(args), out_s...]
    ppermute x17 -> x20, waiting for transfers between devices: 73.7 us -> 29.2 us  [partner(): lax.ppermute(block, AXES, [(low, low ^ flip) for low in range(count)])]
    another operation x17 -> x3, local copies, waits for them, and re-layouts: 20.8 us -> 0.01 us  [per_device(): stacked = jnp.stack(top_pieces)]
    dot_general x21 -> x0, matrix products: 19.5 us -> none  [the longest x3 7.03 us: per_device(): projected = jnp.dot(basis_rows.T, remain, precision=highest)]
    another operation x26 -> x0, matrix products: 13.5 us -> none  [the longest x14 8.92 us: per_device(): solved = jax.scipy.linalg.cho_solve((lower_leaf, True), columns)]
    ppermute x17 -> x20, starting transfers between devices: 20.6 us -> 32.7 us  [partner(): lax.ppermute(block, AXES, [(low, low ^ flip) for low in range(count)])]
  transfers between devices with their start and end apart: 17 -> 20, of which waited for: 14 -> 9; matrix products, arithmetic and copies ran while one was open for 19% -> 3% of each run, Pallas kernels for 0% -> 59%
where the time goes in v1:
time: 235 us
  Pallas kernels  161 us (69%)
  starting transfers between devices  32.7 us (14%)
  waiting for transfers between devices  29.2 us (12%)
  local copies, waits for them, and re-layouts  7.29 us (3%)
  other arithmetic  4.63 us (2%)
    pallas_call x9, Pallas kernels, call(): pl.pallas_call(kernel, out_shape=outs, in_specs=[VMEM] * len(args), out_s...  161 us
    ppermute x20, starting transfers between devices, partner(): lax.ppermute(block, AXES, [(low, low ^ flip) for low in range(count)])  32.7 us
    ppermute x20, waiting for transfers between devices, partner(): lax.ppermute(block, AXES, [(low, low ^ flip) for low in range(count)])  29.2 us
  transfers between devices with their start and end apart: 20, of which 9 were waited for; matrix products, arithmetic and copies ran while one was open for 3% of the time, Pallas kernels for 59%

profile of v1, /device:TPU:0, one launch (start us, length us, event | category | flops | bytes accessed | tf_op | source)
XLA Modules:
  0.0 235.0 jit_solution(6257924573928575316)
XLA Ops:
  0.0 0.7 constant_dynamic-update-slice_fusion.1
  1.2 2.5 %collective-permute-start.4 = (f32[40,128]{1,0:T(8,128)S(1)}, f32[40,128]{1,0:T(8,128)S(1)}, u32[]{:S(2)}, u32[]{:S(2)}) collective-permute-start(f32[40,128]{1,0:T(8,128)S(1)} %constant_dynamic-update-slice_fusion), channel_id=1, source_target_pairs={{0,2},{1,3},{2,0},{3,1},{4,6},{5,7},{6,4},{7,5},{8,10},{9,11},{10,... | collective-permute-start | bytes 61448 | tf_op jit(solution)/shard_map/ppermute | solution.py:19
  3.8 130.4 %leaf.1 = (f32[512,512]{1,0:T(8,128)}, f32[384,512]{1,0:T(8,128)}, f32[2,384,128]{2,1,0:T(8,128)}) custom-call(f32[512,512]{1,0:T(8,128)} %d_ref.1, f32[512,384]{1,0:T(8,128)} %u_ref.1, f32[128,128]{1,0:T(8,128)} %g_ref.1), custom_call_target="tpu_custom_call" | custom-call | tf_op jit(solution)/shard_map/leaf/pallas_call | solution.py:200
  134.2 0.9 slice_bitcast_fusion
  135.3 3.8 %project.1 = f32[4,384,128]{2,1,0:T(8,128)} custom-call(f32[384,512]{1,0:T(8,128)} %get-tuple-element.25.yut_ref, f32[512,512]{1,0:T(8,128)} %rhs_ref.3), custom_call_target="tpu_custom_call" | custom-call | tf_op jit(solution)/shard_map/project/pallas_call | solution.py:200
  139.1 1.1 fusion.3
  142.6 1.8 collective-permute-start.1
  144.7 5.6 %collective-permute-done.1 = f32[384,128]{1,0:T(8,128)S(1)} collective-permute-done((f32[384,128]{1,0:T(8,128)S(1)}, f32[384,128]{1,0:T(8,128)S(1)}, u32[]{:S(2)}, u32[]{:S(2)}) %collective-permute-start.1) | collective-permute-done | bytes 196640 | tf_op jit(solution)/shard_map/ppermute | solution.py:19
  150.5 3.5 %collective-permute-done.14 = f32[384,128]{1,0:T(8,128)S(1)} collective-permute-done((f32[384,128]{1,0:T(8,128)S(1)}, f32[384,128]{1,0:T(8,128)S(1)}, u32[]{:S(2)}, u32[]{:S(2)}) %collective-permute-start.14) | collective-permute-done | bytes 196640 | tf_op jit(solution)/shard_map/ppermute | solution.py:19
  154.0 0.7 fusion.2.p_ref
  155.4 5.0 %lift_zero.1 = (f32[192,128]{1,0:T(8,128)}, f32[128,128]{1,0:T(8,128)}, f32[128,128]{1,0:T(8,128)}, f32[128,256]{1,0:T(8,128)}, f32[128,256]{1,0:T(8,128)}, /*index=5*/f32[128,128]{1,0:T(8,128)}) custom-call(f32[384,128]{1,0:T(8,128)} %copy-done.2, f32[384,128]{1,0:T(8,128)} %copy-done.6, f32[32,128]{1,0:T(8,128)} %refs_0_.1, f32[32,128]{1,0:T(8,128)} %slice.56.refs_1_, ...), custom_call_target="tpu_custom_call" | custom-call | tf_op jit(solution)/shard_map/lift_zero/pallas_call | solution.py:200
  160.4 2.6 %lift_zero_rhs.1 = (f32[128,128]{1,0:T(8,128)}, f32[256,128]{1,0:T(8,128)}) custom-call(f32[384,128]{1,0:T(8,128)} %fusion.2.p_ref, f32[128,128]{1,0:T(8,128)} %get-tuple-element.29.inv_ref, f32[128,128]{1,0:T(8,128)} %get-tuple-element.30.mat_ref, f32[128,256]{1,0:T(8,128)} %get-tuple-element.31.link_ref, f32[128,128]{1,0:T(8,128)} %get-tuple-element.32.next_ref.g1_ref), custom_call_target="tpu_custom_call" | custom-call | tf_op jit(solution)/shard_map/lift_zero_rhs/pallas_call | solution.py:200
  163.0 16.4 %collective-permute-start.15 = (f32[256,128]{1,0:T(8,128)}, f32[256,128]{1,0:T(8,128)S(1)}, u32[]{:S(2)}, u32[]{:S(2)}) collective-permute-start(f32[256,128]{1,0:T(8,128)} %get-tuple-element.33), channel_id=1, source_target_pairs={{0,4},{1,5},{2,6},{3,7},{4,0},{5,1},{6,2},{7,3},{8,12},{9,13},{10,... | collective-permute-start | bytes 393224 | tf_op jit(solution)/shard_map/ppermute | solution.py:19
  179.5 5.4 %collective-permute-done.6 = f32[192,128]{1,0:T(8,128)S(1)} collective-permute-done((f32[192,128]{1,0:T(8,128)S(1)}, f32[192,128]{1,0:T(8,128)S(1)}, u32[]{:S(2)}, u32[]{:S(2)}) %collective-permute-start.6) | collective-permute-done | bytes 98336 | tf_op jit(solution)/shard_map/ppermute | solution.py:19
  184.9 1.9 collective-permute-start.7
  187.1 3.2 %collective-permute-done.7 = f32[192,128]{1,0:T(8,128)S(1)} collective-permute-done((f32[192,128]{1,0:T(8,128)S(1)}, f32[192,128]{1,0:T(8,128)S(1)}, u32[]{:S(2)}, u32[]{:S(2)}) %collective-permute-start.7) | collective-permute-done | bytes 98336 | tf_op jit(solution)/shard_map/ppermute | solution.py:19
  190.4 1.3 collective-permute-start.10
  191.7 1.7 collective-permute-start.11
  194.6 1.7 collective-permute-done.11.refs_3_
  196.3 0.8 collective-permute-done.9.refs_1_
  198.4 4.4 %lift_one.1 = (f32[128,128]{1,0:T(8,128)}, f32[128,128]{1,0:T(8,128)}, f32[128,128]{1,0:T(8,128)}, f32[128,128]{1,0:T(8,128)}, f32[128,128]{1,0:T(8,128)}, /*index=5*/f32[128,128]{1,0:T(8,128)}) custom-call(f32[192,128]{1,0:T(8,128)} %copy-done.5, f32[192,128]{1,0:T(8,128)} %copy-done.8, f32[32,128]{1,0:T(8,128)} %copy-done.11, f32[32,128]{1,0:T(8,128)} %copy-done.14, ...), custom_call_target="tpu_custom_call" | custom-call | tf_op jit(solution)/shard_map/lift_one/pallas_call | solution.py:200
  202.8 2.5 %lift_one_rhs.1 = (f32[128,128]{1,0:T(8,128)}, f32[128,128]{1,0:T(8,128)}) custom-call(f32[256,128]{1,0:T(8,128)} %add.75.p_ref, f32[128,128]{1,0:T(8,128)} %get-tuple-element.34.inv_ref, f32[128,128]{1,0:T(8,128)} %get-tuple-element.35.mat_ref, f32[128,128]{1,0:T(8,128)} %get-tuple-element.36.link_ref, f32[128,128]{1,0:T(8,128)} %get-tuple-element.37.next_ref.g2_ref), custom_call_target="tpu_custom_call" | custom-call | tf_op jit(solution)/shard_map/lift_one_rhs/pallas_call | solution.py:200
  205.3 2.6 %collective-permute-start.17 = (f32[128,128]{1,0:T(8,128)}, f32[128,128]{1,0:T(8,128)S(1)}, u32[]{:S(2)}, u32[]{:S(2)}) collective-permute-start(f32[128,128]{1,0:T(8,128)} %get-tuple-element.38), channel_id=1, source_target_pairs={{0,16},{1,17},{2,18},{3,19},{4,20},{5,21},{6,22},{7,23},{8,24},{9,... | collective-permute-start | bytes 196616 | tf_op jit(solution)/shard_map/ppermute | solution.py:19
  208.2 4.4 %collective-permute-done.17 = f32[128,128]{1,0:T(8,128)S(1)} collective-permute-done((f32[128,128]{1,0:T(8,128)}, f32[128,128]{1,0:T(8,128)S(1)}, u32[]{:S(2)}, u32[]{:S(2)}) %collective-permute-start.17) | collective-permute-done | bytes 65568 | tf_op jit(solution)/shard_map/ppermute | solution.py:19
  212.6 1.5 add.76.p_ref
  214.8 4.8 %top.1.c0_ref = f32[384,128]{1,0:T(8,128)} custom-call(f32[128,128]{1,0:T(8,128)} %add.68.w_ref, f32[128,128]{1,0:T(8,128)} %add.76.p_ref, f32[128,128]{1,0:T(8,128)} %get-tuple-element.32.next_ref.g1_ref, f32[128,128]{1,0:T(8,128)} %get-tuple-element.37.next_ref.g2_ref, f32[128,128]{1,0:T(8,128)} %get-tuple-element.39.f0r_ref, ...), custom_call_target="tpu_custom_call" | custom-call | tf_op jit(solution)/shard_map/top/pallas_call | solution.py:200
  219.6 1.5 collective-permute-start.18
  221.1 4.4 %collective-permute-done.18.c2_ref = f32[384,128]{1,0:T(8,128)S(1)} collective-permute-done((f32[384,128]{1,0:T(8,128)}, f32[384,128]{1,0:T(8,128)S(1)}, u32[]{:S(2)}, u32[]{:S(2)}) %collective-permute-start.18) | collective-permute-done | bytes 196640 | tf_op jit(solution)/shard_map/ppermute | solution.py:19
  225.5 1.0 pad_maximum_fusion.1
  226.6 3.5 %solve.1.y_ref = f32[512,512]{1,0:T(8,128)} custom-call(f32[512,512]{1,0:T(8,128)} %get-tuple-element.24.dinv_ref, f32[512,512]{1,0:T(8,128)} %rhs_ref.3), custom_call_target="tpu_custom_call" | custom-call | tf_op jit(solution)/shard_map/solve/pallas_call | solution.py:200
  230.1 0.7 copy-done.3
  230.9 4.1 %finish.1 = f32[512,512]{1,0:T(8,128)} custom-call(f32[512,512]{1,0:T(8,128)} %solve.1.y_ref, f32[384,512]{1,0:T(8,128)} %get-tuple-element.25.yut_ref, f32[384,128]{1,0:T(8,128)} %top.1.c0_ref, f32[384,128]{1,0:T(8,128)} %copy-done.1, f32[2,384,128]{2,1,0:T(8,128)} %copy-done.3), custom_call_target="tpu_custom_call" | custom-call | tf_op jit(solution)/shard_map/finish/pallas_call | solution.py:200
  (74 shorter events, 8.2 us)
Async XLA Ops:
  0.7 140.0 %collective-permute-start.3 = (f32[40,128]{1,0:T(8,128)S(1)}, f32[40,128]{1,0:T(8,128)S(1)}, u32[]{:S(2)}, u32[]{:S(2)}) collective-permute-start(f32[40,128]{1,0:T(8,128)S(1)} %constant_dynamic-update-slice_fusion), channel_id=1, source_target_pairs={{0,1},{1,0},{2,3},{3,2},{4,5},{5,4},{6,7},{7,6},{8,9},{9,8},{10,11... | collective-permute-start | bytes 61448 | tf_op jit(solution)/shard_map/ppermute | solution.py:19
  1.2 140.1 %collective-permute-start.4 = (f32[40,128]{1,0:T(8,128)S(1)}, f32[40,128]{1,0:T(8,128)S(1)}, u32[]{:S(2)}, u32[]{:S(2)}) collective-permute-start(f32[40,128]{1,0:T(8,128)S(1)} %constant_dynamic-update-slice_fusion), channel_id=1, source_target_pairs={{0,2},{1,3},{2,0},{3,1},{4,6},{5,7},{6,4},{7,5},{8,10},{9,11},{10,... | collective-permute-start | bytes 61448 | tf_op jit(solution)/shard_map/ppermute | solution.py:19
  3.8 138.1 %collective-permute-start.5 = (f32[40,128]{1,0:T(8,128)S(1)}, f32[40,128]{1,0:T(8,128)S(1)}, u32[]{:S(2)}, u32[]{:S(2)}) collective-permute-start(f32[40,128]{1,0:T(8,128)S(1)} %constant_dynamic-update-slice_fusion), channel_id=1, source_target_pairs={{0,3},{1,2},{2,1},{3,0},{4,7},{5,6},{6,5},{7,4},{8,11},{9,10},{10,... | collective-permute-start | bytes 61448 | tf_op jit(solution)/shard_map/ppermute | solution.py:19
  135.1 7.4 %collective-permute-start = (f32[384,128]{1,0:T(8,128)S(1)}, f32[384,128]{1,0:T(8,128)S(1)}, u32[]{:S(2)}, u32[]{:S(2)}) collective-permute-start(f32[384,128]{1,0:T(8,128)S(1)} %slice_bitcast_fusion), channel_id=1, source_target_pairs={{0,1},{1,0},{2,3},{3,2},{4,5},{5,4},{6,7},{7,6},{8,9},{9,8},{10,11... | collective-permute-start | bytes 589832 | tf_op jit(solution)/shard_map/ppermute | solution.py:19
  139.1 3.4 %copy-start.4 = (f32[2,384,128]{2,1,0:T(8,128)S(1)}, f32[2,384,128]{2,1,0:T(8,128)}, u32[]{:S(2)}) copy-start(f32[2,384,128]{2,1,0:T(8,128)} %get-tuple-element.26) | copy-start | bytes 1179652
  140.2 4.1 %copy-start = (f32[4,384,128]{2,1,0:T(8,128)S(1)}, f32[4,384,128]{2,1,0:T(8,128)}, u32[]{:S(2)}) copy-start(f32[4,384,128]{2,1,0:T(8,128)} %project.1) | copy-start | bytes 2359300
  140.3 4.1 %collective-permute-start.13 = (f32[2,384,128]{2,1,0:T(8,128)S(1)}, f32[2,384,128]{2,1,0:T(8,128)S(1)}, u32[]{:S(2)}, u32[]{:S(2)}) collective-permute-start(f32[2,384,128]{2,1,0:T(8,128)S(1)} %pad_maximum_fusion), channel_id=1, source_target_pairs={{0,1},{1,0},{2,3},{3,2},{4,5},{5,4},{6,7},{7,6},{8,9},{9,8},{10,11... | collective-permute-start | bytes 1179656 | tf_op jit(solution)/shard_map/ppermute | solution.py:19
  142.6 7.8 %collective-permute-start.1 = (f32[384,128]{1,0:T(8,128)S(1)}, f32[384,128]{1,0:T(8,128)S(1)}, u32[]{:S(2)}, u32[]{:S(2)}) collective-permute-start(f32[384,128]{1,0:T(8,128)S(1)} %bitcast_add_fusion), channel_id=1, source_target_pairs={{0,2},{1,3},{2,0},{3,1},{4,6},{5,7},{6,4},{7,5},{8,10},{9,11},{10,... | collective-permute-start | bytes 589832 | tf_op jit(solution)/shard_map/ppermute | solution.py:19
  144.4 9.6 %collective-permute-start.14 = (f32[384,128]{1,0:T(8,128)S(1)}, f32[384,128]{1,0:T(8,128)S(1)}, u32[]{:S(2)}, u32[]{:S(2)}) collective-permute-start(f32[384,128]{1,0:T(8,128)S(1)} %fusion), channel_id=1, source_target_pairs={{0,2},{1,3},{2,0},{3,1},{4,6},{5,7},{6,4},{7,5},{8,10},{9,11},{10,... | collective-permute-start | bytes 589832 | tf_op jit(solution)/shard_map/ppermute | solution.py:19
  150.4 4.3 %copy-start.2 = (f32[384,128]{1,0:T(8,128)}, f32[384,128]{1,0:T(8,128)S(1)}, u32[]{:S(2)}) copy-start(f32[384,128]{1,0:T(8,128)S(1)} %add.59.mine_ref) | copy-start | bytes 589828
  150.4 4.3 %collective-permute-start.2 = (f32[384,128]{1,0:T(8,128)S(1)}, f32[384,128]{1,0:T(8,128)S(1)}, u32[]{:S(2)}, u32[]{:S(2)}) collective-permute-start(f32[384,128]{1,0:T(8,128)S(1)} %add.59.mine_ref), channel_id=1, source_target_pairs={{0,1},{1,0},{2,3},{3,2},{4,5},{5,4},{6,7},{7,6},{8,9},{9,8},{10,11... | collective-permute-start | bytes 589832 | tf_op jit(solution)/shard_map/ppermute | solution.py:19
  160.4 19.0 %copy-start.9 = (f32[192,128]{1,0:T(8,128)S(1)}, f32[192,128]{1,0:T(8,128)}, u32[]{:S(2)}) copy-start(f32[192,128]{1,0:T(8,128)} %get-tuple-element.27) | copy-start | bytes 294916
  163.0 23.8 %collective-permute-start.15 = (f32[256,128]{1,0:T(8,128)}, f32[256,128]{1,0:T(8,128)S(1)}, u32[]{:S(2)}, u32[]{:S(2)}) collective-permute-start(f32[256,128]{1,0:T(8,128)} %get-tuple-element.33), channel_id=1, source_target_pairs={{0,4},{1,5},{2,6},{3,7},{4,0},{5,1},{6,2},{7,3},{8,12},{9,13},{10,... | collective-permute-start | bytes 393224 | tf_op jit(solution)/shard_map/ppermute | solution.py:19
  179.4 5.5 %collective-permute-start.6 = (f32[192,128]{1,0:T(8,128)S(1)}, f32[192,128]{1,0:T(8,128)S(1)}, u32[]{:S(2)}, u32[]{:S(2)}) collective-permute-start(f32[192,128]{1,0:T(8,128)S(1)} %copy-done.9), channel_id=1, source_target_pairs={{0,4},{1,5},{2,6},{3,7},{4,0},{5,1},{6,2},{7,3},{8,12},{9,13},{10,... | collective-permute-start | bytes 294920 | tf_op jit(solution)/shard_map/ppermute | solution.py:19
  179.5 7.3 %copy-start.7 = (f32[256,128]{1,0:T(8,128)S(1)}, f32[256,128]{1,0:T(8,128)}, u32[]{:S(2)}) copy-start(f32[256,128]{1,0:T(8,128)} %get-tuple-element.33) | copy-start | bytes 393220
  184.9 5.4 %collective-permute-start.7 = (f32[192,128]{1,0:T(8,128)S(1)}, f32[192,128]{1,0:T(8,128)S(1)}, u32[]{:S(2)}, u32[]{:S(2)}) collective-permute-start(f32[192,128]{1,0:T(8,128)S(1)} %add.60), channel_id=1, source_target_pairs={{0,8},{1,9},{2,10},{3,11},{4,12},{5,13},{6,14},{7,15},{8,0},{9,1},... | collective-permute-start | bytes 294920 | tf_op jit(solution)/shard_map/ppermute | solution.py:19
  186.8 7.2 %collective-permute-start.16 = (f32[256,128]{1,0:T(8,128)S(1)}, f32[256,128]{1,0:T(8,128)S(1)}, u32[]{:S(2)}, u32[]{:S(2)}) collective-permute-start(f32[256,128]{1,0:T(8,128)S(1)} %add.74), channel_id=1, source_target_pairs={{0,8},{1,9},{2,10},{3,11},{4,12},{5,13},{6,14},{7,15},{8,0},{9,1},... | collective-permute-start | bytes 393224 | tf_op jit(solution)/shard_map/ppermute | solution.py:19
  190.3 4.3 %copy-start.5 = (f32[192,128]{1,0:T(8,128)}, f32[192,128]{1,0:T(8,128)S(1)}, u32[]{:S(2)}) copy-start(f32[192,128]{1,0:T(8,128)S(1)} %add.61.mine_ref) | copy-start | bytes 294916
  190.3 6.9 %collective-permute-start.8 = (f32[192,128]{1,0:T(8,128)S(1)}, f32[192,128]{1,0:T(8,128)S(1)}, u32[]{:S(2)}, u32[]{:S(2)}) collective-permute-start(f32[192,128]{1,0:T(8,128)S(1)} %add.61.mine_ref), channel_id=1, source_target_pairs={{0,1},{1,0},{2,3},{3,2},{4,5},{5,4},{6,7},{7,6},{8,9},{9,8},{10,11... | collective-permute-start | bytes 294920 | tf_op jit(solution)/shard_map/ppermute | solution.py:19
  190.4 4.2 %copy-start.11 = (f32[32,128]{1,0:T(8,128)}, f32[32,128]{1,0:T(8,128)S(1)}, u32[]{:S(2)}) copy-start(f32[32,128]{1,0:T(8,128)S(1)} %pad_maximum_fusion.3.refs_0_) | copy-start | bytes 49156
  190.4 4.2 %collective-permute-start.10 = (f32[32,128]{1,0:T(8,128)S(1)}, f32[32,128]{1,0:T(8,128)S(1)}, u32[]{:S(2)}, u32[]{:S(2)}) collective-permute-start(f32[32,128]{1,0:T(8,128)S(1)} %pad_maximum_fusion.3.refs_0_), channel_id=1, source_target_pairs={{0,8},{1,9},{2,10},{3,11},{4,12},{5,13},{6,14},{7,15},{8,0},{9,1},... | collective-permute-start | bytes 49160 | tf_op jit(solution)/shard_map/ppermute | solution.py:19
  191.7 4.6 %collective-permute-start.11 = (f32[32,128]{1,0:T(8,128)S(1)}, f32[32,128]{1,0:T(8,128)S(1)}, u32[]{:S(2)}, u32[]{:S(2)}) collective-permute-start(f32[32,128]{1,0:T(8,128)S(1)} %pad_maximum_fusion.3.refs_0_), channel_id=1, source_target_pairs={{0,12},{1,13},{2,14},{3,15},{4,8},{5,9},{6,10},{7,11},{8,4},{9,5},... | collective-permute-start | bytes 49160 | tf_op jit(solution)/shard_map/ppermute | solution.py:19
  193.4 3.7 %collective-permute-start.9 = (f32[32,128]{1,0:T(8,128)S(1)}, f32[32,128]{1,0:T(8,128)S(1)}, u32[]{:S(2)}, u32[]{:S(2)}) collective-permute-start(f32[32,128]{1,0:T(8,128)S(1)} %pad_maximum_fusion.3.refs_0_), channel_id=1, source_target_pairs={{0,4},{1,5},{2,6},{3,7},{4,0},{5,1},{6,2},{7,3},{8,12},{9,13},{10,... | collective-permute-start | bytes 49160 | tf_op jit(solution)/shard_map/ppermute | solution.py:19
  194.6 2.6 %copy-start.12 = (f32[32,128]{1,0:T(8,128)}, f32[32,128]{1,0:T(8,128)S(1)}, u32[]{:S(2)}) copy-start(f32[32,128]{1,0:T(8,128)S(1)} %collective-permute-done.10.refs_2_) | copy-start | bytes 49156
  196.3 0.9 copy-start.13
  202.8 5.1 %copy-start.10 = (f32[128,128]{1,0:T(8,128)S(1)}, f32[128,128]{1,0:T(8,128)}, u32[]{:S(2)}) copy-start(f32[128,128]{1,0:T(8,128)} %get-tuple-element.28) | copy-start | bytes 196612
  205.3 7.3 %collective-permute-start.17 = (f32[128,128]{1,0:T(8,128)}, f32[128,128]{1,0:T(8,128)S(1)}, u32[]{:S(2)}, u32[]{:S(2)}) collective-permute-start(f32[128,128]{1,0:T(8,128)} %get-tuple-element.38), channel_id=1, source_target_pairs={{0,16},{1,17},{2,18},{3,19},{4,20},{5,21},{6,22},{7,23},{8,24},{9,... | collective-permute-start | bytes 196616 | tf_op jit(solution)/shard_map/ppermute | solution.py:19
  207.9 6.3 %collective-permute-start.12 = (f32[128,128]{1,0:T(8,128)S(1)}, f32[128,128]{1,0:T(8,128)S(1)}, u32[]{:S(2)}, u32[]{:S(2)}) collective-permute-start(f32[128,128]{1,0:T(8,128)S(1)} %copy-done.10), channel_id=1, source_target_pairs={{0,16},{1,17},{2,18},{3,19},{4,20},{5,21},{6,22},{7,23},{8,24},{9,... | collective-permute-start | bytes 196616 | tf_op jit(solution)/shard_map/ppermute | solution.py:19
  219.6 5.9 %collective-permute-start.18 = (f32[384,128]{1,0:T(8,128)}, f32[384,128]{1,0:T(8,128)S(1)}, u32[]{:S(2)}, u32[]{:S(2)}) collective-permute-start(f32[384,128]{1,0:T(8,128)} %top.1.c0_ref), channel_id=1, source_target_pairs={{0,2},{1,3},{2,0},{3,1},{4,6},{5,7},{6,4},{7,5},{8,10},{9,11},{10,... | collective-permute-start | bytes 589832 | tf_op jit(solution)/shard_map/ppermute | solution.py:19
  225.5 1.0 copy-start.1
  226.5 3.6 %collective-permute-start.19 = (f32[2,384,128]{2,1,0:T(8,128)S(1)}, f32[2,384,128]{2,1,0:T(8,128)S(1)}, u32[]{:S(2)}, u32[]{:S(2)}) collective-permute-start(f32[2,384,128]{2,1,0:T(8,128)S(1)} %pad_maximum_fusion.1), channel_id=1, source_target_pairs={{0,1},{1,0},{2,3},{3,2},{4,5},{5,4},{6,7},{7,6},{8,9},{9,8},{10,11... | collective-permute-start | bytes 1179656 | tf_op jit(solution)/shard_map/ppermute | solution.py:19
  230.1 0.7 copy-start.3
  (4 other events, 2.7 us)
